TPU v7x, 32 devices: a whole 2x2x4 slice. The times are simulated.
32 devices in a mesh: groups: 2 (over y), mom: 4 (over z), tm: 4 (over x, core).
Axes of the slice: x: 2, y: 2, z: 4, core: 2. Of those that a mesh axis runs over, the one named last changes fastest.
Arguments:
- panel_start: float32 [256, 4, 64, 512], P('mom', 'groups', None, 'tm'), parts along dimension 1, may hold values from -6 to 6
- block_guess: float32 [256, 4, 64, 128], P('mom', 'groups', 'tm'), parts along dimension 1, may hold values from -6 to 6
- coupling: float32 [2], P('groups'), parts along dimension 0, may hold values from 0.3 to 0.6
- slab_owner: int32 [8], P('groups'), parts along dimension 0, may hold values from 0 to 3, each once
- expiring: int32 [2], P('groups'), parts along dimension 0, may hold values from 0 to 3
- ordering: int32 [256], replicated, may hold values from 0 to 255, each once
Outputs:
- history_out: float32 [256, 4, 64, 512], P('mom', 'groups', None, 'tm'), parts along dimension 1
There are 2 independent parts, one for each index of `groups`. A program takes and returns all parts, laid end to end along the dimension named above; an argument that names none is the same for every part. Nothing has to cross between parts.
Inputs may be any that keep to these rules, and one draw needn't show every extreme that they name: `slab_owner`: entry s is the column block that holds history slab s; each block once. `ordering`: entry j is qx * 16 + qy for the momentum of stored row j; each momentum once.
All inputs are finite; a program needn't handle non-finite values.
Results may differ from a plain program's by a relative error of at most 0.0001.
Values sent between devices are 32-bit elements; how exact they have to be, the bound alone decides.
A program may use at most 128 MiB of HBM per device.

v0:
```python
import math

import jax
import jax.numpy as jnp
from jax import lax
from jax.sharding import PartitionSpec as P

LSIDE = 16
K = 256
PANEL = 64
PASSES = 2


def product(left, right):
    return jnp.dot(left, right, precision=lax.Precision.HIGHEST, preferred_element_type=jnp.float32)


def contract(pattern, left, right):
    return jnp.einsum(
        pattern, left, right, precision=lax.Precision.HIGHEST, preferred_element_type=jnp.float32
    )


def tables(ordering):
    site_index = jnp.arange(K, dtype=jnp.int32)
    site_x = site_index // LSIDE
    site_y = site_index % LSIDE
    mom_x = ordering // LSIDE
    mom_y = ordering % LSIDE
    phases = (site_x[:, None] * mom_x[None, :] + site_y[:, None] * mom_y[None, :]) % LSIDE
    angles = phases.astype(jnp.float32) * (2.0 * math.pi / LSIDE)
    mirror = -site_x % LSIDE * LSIDE + -site_y % LSIDE
    return (jnp.cos(angles) / LSIDE, jnp.sin(angles) / LSIDE, mirror)


def site_sigma(joined, cos_table, sin_table, mirror, strength):
    layout = joined.shape
    flat = joined.reshape(K, -1)
    with_cos = product(cos_table, flat).reshape(layout)
    with_sin = product(sin_table, flat).reshape(layout)
    site_re = with_cos[..., :PANEL] - with_sin[..., PANEL:]
    site_im = with_cos[..., PANEL:] + with_sin[..., :PANEL]
    other_re = site_re[:, ::-1]
    other_im = site_im[:, ::-1]
    pair_re = site_re * other_re - site_im * other_im
    pair_im = site_re * other_im + site_im * other_re
    back_re = jnp.take(other_re, mirror, axis=0)
    back_im = jnp.take(other_im, mirror, axis=0)
    sig_re = -strength * (pair_re * back_re + pair_im * back_im)
    sig_im = -strength * (pair_im * back_re - pair_re * back_im)
    sig_flat = jnp.concatenate([sig_re, sig_im], axis=-1).reshape(K, -1)
    back_cos = product(cos_table.T, sig_flat).reshape(layout)
    back_sin = product(sin_table.T, sig_flat).reshape(layout)
    out_re = back_cos[..., :PANEL] + back_sin[..., PANEL:]
    out_im = back_cos[..., PANEL:] - back_sin[..., :PANEL]
    return jnp.concatenate([out_re, out_im], axis=-1)


def rotated(joined):
    return jnp.concatenate([-joined[..., PANEL:], joined[..., :PANEL]], axis=-1)


def partial_conv(weighted, stacked):
    return -contract("ksau,ksbu->ksab", weighted, stacked)


def own_block(guess, conv, step_scale):
    stacked = jnp.concatenate([conv, rotated(conv)], axis=2)
    return guess + step_scale * contract("ksab,ksbc->ksac", guess, stacked)


def body(panel_start, block_guess, coupling, slab_owner, expiring, ordering):
    slab_count = lax.axis_size("tm")
    own_index = lax.axis_index("tm")
    cos_table, sin_table, mirror = tables(ordering)
    blocks = jnp.arange(slab_count, dtype=jnp.int32)
    slab_mine = jnp.sum(blocks * (slab_owner == own_index).astype(jnp.int32))
    position = (slab_mine - expiring[0]) % slab_count
    window = slab_count * PANEL
    times = position * PANEL + jnp.arange(PANEL, dtype=jnp.int32)
    weights = jnp.exp(-1.5 * (window - 1 - times).astype(jnp.float32) / window) / math.sqrt(window)
    weights_both = jnp.concatenate([weights, weights])
    strength = coupling[0] * coupling[0]
    step_scale = 1.0 / math.sqrt(PANEL)
    guess_full = lax.all_gather(block_guess, "tm", axis=2, tiled=True)
    current = panel_start
    conv = None
    for sweep in range(PASSES):
        exchanged = lax.all_to_all(current, "mom", split_axis=2, concat_axis=0, tiled=True)
        sig_sites = site_sigma(exchanged, cos_table, sin_table, mirror, strength)
        returned = lax.all_to_all(sig_sites, "mom", split_axis=0, concat_axis=2, tiled=True)
        weighted = returned * weights_both
        stacked = jnp.concatenate([current, rotated(current)], axis=2)
        conv = lax.psum(partial_conv(weighted, stacked), "tm")
        current = panel_start + step_scale * contract("ksab,ksbu->ksau", conv, stacked)
    block = own_block(guess_full, conv, step_scale)
    owner_expiring = jnp.sum(slab_owner * (blocks == expiring[0]).astype(jnp.int32))
    return jnp.where(own_index == owner_expiring, block, current)


def solution(mesh):
    return jax.shard_map(
        body,
        mesh=mesh,
        in_specs=(
            P("mom", "groups", None, "tm"),
            P("mom", "groups", "tm", None),
            P("groups"),
            P("groups"),
            P("groups"),
            P(),
        ),
        out_specs=P("mom", "groups", None, "tm"),
        check_vma=False,
    )
```

profile of v0, /device:TPU:26, one launch (start us, length us, event | category | flops | bytes accessed | tf_op | source)
XLA Modules:
  0.0 877.9 jit_solution(12300599067651321247)
XLA Ops:
  6.5 6.6 copy.58
  13.2 5.2 all-to-all-start
  19.1 90.4 %all-to-all-done = f32[64,2,64,128]{3,0,1,2:T(8,128)} async-done(((f32[64,2,64,128]{3,0,1,2:T(8,128)}), f32[64,2,64,128]{3,0,1,2:T(8,128)}, u32[]{:S(2)}, u32[]{:S(2)}) %all-to-all-start) | async-done | bytes 4194336 | tf_op jit(solution)/shard_map/all_to_all | solution.py:89
  109.5 6.6 copy.81
  116.2 4.9 reshape.62
  121.1 5.8 copy.60
  126.9 7.0 fusion.26
  133.9 4.7 fusion.32
  138.6 2.2 slice_subtract_fusion.3
  140.8 1.5 rev.12
  142.3 5.5 copy.61
  147.9 4.9 gather_fusion
  152.8 5.1 copy.62
  157.9 3.1 rev.13
  161.1 5.5 copy.63
  166.6 4.9 gather_fusion.1
  171.6 4.6 copy.64
  176.1 4.7 add_multiply_fusion.1
  180.8 4.7 fusion.13
  185.5 5.2 fusion.14
  191.8 2.5 pad_maximum_fusion
  194.3 5.7 copy.65
  200.0 7.3 all-to-all-start.1
  209.5 8.1 slice_negate_fusion.2
  217.6 80.1 %all-to-all-done.1 = f32[256,2,16,128]{3,2,1,0:T(8,128)} async-done(((f32[256,2,16,128]{3,2,1,0:T(8,128)}), f32[256,2,16,128]{3,2,1,0:T(8,128)}, u32[]{:S(2)}, u32[]{:S(2)}) %all-to-all-start.1) | async-done | bytes 4194336 | tf_op jit(solution)/shard_map/all_to_all | solution.py:91
  297.8 3.0 copy.66
  301.3 1.8 copy-done
  303.0 1.2 copy-done.6
  304.2 17.3 %fusion.15 = f32[64,2,64,128]{3,2,1,0:T(8,128)} fusion(f32[64,2,64,128]{3,2,1,0:T(8,128)S(1)} %bitcast_multiply_fusion.1, f32[64,2,64,64]{3,2,1,0:T(8,128)S(1)} %copy-done.7, f32[64,2,64,64]{3,2,1,0:T(8,128)S(1)} %copy-done.6, f32[64,2,64,128]{3,2,1,0:T(8,128)S(1)} %copy-done), kind=kOutput, calls=%fused_computation.50 | convolution fusion | flops 1615855616 | bytes 16777216 | tf_op jit(solution)/shard_map/ksau,ksbu->ksab/dot_general | solution.py:19
  321.6 85.8 %all-reduce.3.cloned.1.call-done = f32[64,2,64,128]{3,2,1,0:T(8,128)} async-done(((f32[64,2,64,128]{3,2,1,0:T(8,128)}), f32[64,2,64,128]{3,2,1,0:T(8,128)}) %all-reduce.3.cloned.1.call-update) | async-done | bytes 4194320 | tf_op jit(solution)/shard_map/psum | solution.py:94
  407.4 15.2 %multiply_add_fusion = f32[64,2,64,128]{3,2,1,0:T(8,128)S(1)} fusion(f32[64,2,64,128]{3,2,1,0:T(8,128)} %param.8, f32[64,2,64,128]{3,2,1,0:T(8,128)} %all-reduce.3.cloned.1.call-done, f32[64,2,64,64]{3,2,1,0:T(8,128)} %get-tuple-element.25, f32[64,2,64,64]{3,2,1,0:T(8,128)} %get-tuple-element.24), kind=kOutput, calls=%fused_computation.24 | convolution fusion | flops 1616904192 | bytes 16777216 | tf_op jit(solution)/shard_map/ksab,ksbu->ksau/dot_general | solution.py:19
  422.7 3.2 copy.67
  425.9 96.0 %all_to_all.66 = f32[64,2,64,128]{3,1,0,2:T(2,128)S(1)} all-to-all(f32[64,2,64,128]{3,1,0,2:T(2,128)S(1)} %copy.67), channel_id=1, replica_groups=mesh['groups'=2,'mom'=4,'tm'=4] {'mom'}, dimensions={2} | all-to-all | bytes 8388608 | tf_op jit(solution)/shard_map/all_to_all | solution.py:89
  521.9 4.4 copy.80
  526.3 5.0 reshape.64
  531.4 6.0 copy.69
  537.4 7.0 fusion.23
  544.4 4.7 fusion.29
  549.1 2.2 slice_subtract_fusion.1
  551.4 1.5 rev.14
  552.9 5.5 copy.70
  558.4 5.0 gather_fusion.2
  563.5 4.7 copy.71
  568.2 3.2 rev.15
  571.4 5.5 copy.72
  576.9 5.0 gather_fusion.3
  581.9 4.6 copy.73
  586.5 4.7 add_multiply_fusion
  591.2 4.7 fusion.11
  595.9 5.2 fusion.12
  602.2 2.5 pad_maximum_fusion.1
  604.7 5.7 copy.74
  610.3 7.0 all-to-all-start.3
  617.3 8.2 slice_negate_fusion.1
  625.5 81.9 %all-to-all-done.3 = f32[256,2,16,128]{3,2,1,0:T(8,128)} async-done(((f32[256,2,16,128]{3,2,1,0:T(8,128)}), f32[256,2,16,128]{3,2,1,0:T(8,128)}, u32[]{:S(2)}, u32[]{:S(2)}) %all-to-all-start.3) | async-done | bytes 4194336 | tf_op jit(solution)/shard_map/all_to_all | solution.py:91
  707.4 3.0 copy.75
  710.9 1.8 copy-done.2
  712.6 1.2 copy-done.4
  713.8 17.2 %fusion.16 = f32[64,2,64,128]{3,2,1,0:T(8,128)} fusion(f32[64,2,64,128]{3,2,1,0:T(8,128)S(1)} %bitcast_multiply_fusion, f32[64,2,64,64]{3,2,1,0:T(8,128)S(1)} %copy-done.5, f32[64,2,64,64]{3,2,1,0:T(8,128)S(1)} %copy-done.4, f32[64,2,64,128]{3,2,1,0:T(8,128)S(1)} %copy-done.2), kind=kOutput, calls=%fused_computation.51 | convolution fusion | flops 1615855616 | bytes 16777216 | tf_op jit(solution)/shard_map/ksau,ksbu->ksab/dot_general | solution.py:19
  732.5 84.4 %all-reduce.5.cloned.1.call-done = f32[64,2,64,128]{3,2,1,0:T(8,128)} async-done(((f32[64,2,64,128]{3,2,1,0:T(8,128)}), f32[64,2,64,128]{3,2,1,0:T(8,128)}) %all-reduce.5.cloned.1.call-update) | async-done | bytes 4194320 | tf_op jit(solution)/shard_map/psum | solution.py:94
  816.9 13.2 %fusion.7 = f32[64,2,64,128]{3,2,1,0:T(8,128)} fusion(f32[64,2,64,128]{3,2,1,0:T(8,128)} %all-reduce.5.cloned.1.call-done, f32[64,2,64,64]{3,2,1,0:T(8,128)} %get-tuple-element.23, f32[64,2,64,64]{3,2,1,0:T(8,128)} %get-tuple-element.22, f32[64,2,64,128]{3,2,1,0:T(8,128)} %copy-done.1), kind=kOutput, calls=%fused_computation.26 | convolution fusion | flops 1614807040 | bytes 16777216 | tf_op jit(solution)/shard_map/ksab,ksbu->ksau/dot_general | solution.py:19
  830.1 4.7 slice_negate_fusion
  834.9 18.1 %all-gather.2.cloned.1.call-done = f32[64,2,64,128]{3,2,1,0:T(8,128)} async-done(((f32[64,2,16,128]{3,2,1,0:T(8,128)}), f32[64,2,64,128]{3,2,1,0:T(8,128)}) %all-gather.2.cloned.1.call-update) | async-done | bytes 4194320 | tf_op jit(solution)/shard_map/all_gather | solution.py:85
  852.9 18.0 %fusion.6 = f32[64,2,64,128]{3,2,1,0:T(8,128)} fusion(f32[64,2,64,128]{3,2,1,0:T(8,128)} %all-gather.2.cloned.1.call-done, f32[64,2,64,128]{3,2,1,0:T(8,128)} %param.8, f32[64,2,64,128]{3,2,1,0:T(8,128)} %fusion.7, pred[]{:T(512)S(6)} %eq.26, f32[64,2,64,64]{3,2,1,0:T(8,128)} %get-tuple-element.21, f32[64,2,64,64]{3,2,1,0:T(8,128)} %get-tuple-element.20, ...), kind=kOutput, calls=%fused_computation.19 | convolution fusion | flops 1620049920 | bytes 25165824 | tf_op jit(solution)/shard_map/ksab,ksbc->ksac/dot_general | solution.py:19
  (38 shorter events, 4.8 us)
Async XLA Ops:
  13.2 5.9 copy-start.10
  13.2 96.4 %all-to-all-start = ((f32[64,2,64,128]{3,0,1,2:T(8,128)}), f32[64,2,64,128]{3,0,1,2:T(8,128)}, u32[]{:S(2)}, u32[]{:S(2)}) async-start(f32[64,2,64,128]{3,0,1,2:T(8,128)} %copy.58), calls=%async_computation | async-start | bytes 8388608 | tf_op jit(solution)/shard_map/all_to_all | solution.py:89
  126.9 7.1 copy-start.8
  200.0 8.0 copy-start.11
  200.0 97.8 %all-to-all-start.1 = ((f32[256,2,16,128]{3,2,1,0:T(8,128)}), f32[256,2,16,128]{3,2,1,0:T(8,128)}, u32[]{:S(2)}, u32[]{:S(2)}) async-start(f32[256,2,16,128]{3,2,1,0:T(8,128)} %copy.65), calls=%async_computation.1 | async-start | bytes 8388608 | tf_op jit(solution)/shard_map/all_to_all | solution.py:91
  207.3 200.1 %all-reduce.3.cloned.1.call-start = ((), (), s32[]{:S(2)}) async-start(), calls=%async_computation.5 | async-start | bytes 8388608 | tf_op jit(solution)/shard_map/psum | solution.py:94
  297.8 3.5 copy-start.7
  300.7 2.3 copy-start
  300.7 3.5 copy-start.6
  422.7 3.3 copy-start.1
  537.4 7.1 copy-start.9
  610.3 97.0 %all-to-all-start.3 = ((f32[256,2,16,128]{3,2,1,0:T(8,128)}), f32[256,2,16,128]{3,2,1,0:T(8,128)}, u32[]{:S(2)}, u32[]{:S(2)}) async-start(f32[256,2,16,128]{3,2,1,0:T(8,128)} %copy.74), calls=%async_computation.3 | async-start | bytes 8388608 | tf_op jit(solution)/shard_map/all_to_all | solution.py:91
  617.3 199.6 %all-reduce.5.cloned.1.call-start = ((), (), s32[]{:S(2)}) async-start(), calls=%async_computation.6 | async-start | bytes 8388608 | tf_op jit(solution)/shard_map/psum | solution.py:94
  707.4 3.5 copy-start.5
  710.3 2.3 copy-start.2
  710.3 3.5 copy-start.4
  731.1 121.8 %all-gather.2.cloned.1.call-start = ((), (), s32[]{:S(2)}) async-start(), calls=%async_computation.4 | async-start | bytes 5242880 | tf_op jit(solution)/shard_map/all_gather | solution.py:85
  816.9 13.2 %copy-start.3 = (f32[64,2,64,128]{3,2,1,0:T(8,128)S(1)}, f32[64,2,64,128]{3,2,1,0:T(8,128)}, u32[]{:S(2)}) copy-start(f32[64,2,64,128]{3,2,1,0:T(8,128)} %all-reduce.5.cloned.1.call-done) | copy-start | bytes 12582916
Sparse Core Ops, SparseCore 0:
  321.7 85.6 all-reduce.2
  731.2 85.6 all-reduce.4
  818.5 34.4 all-gather.1
where the time goes:
time: 887 us; the launch traced here: 878 us
  waiting for transfers between devices  441 us (50%)
  local copies, waits for them, and re-layouts  136 us (15%)
  matrix products  124 us (14%)
  blocking collectives  96 us (11%)
  other arithmetic  43.8 us (5%)
  starting transfers between devices  19.6 us (2%)
  between operations  16.5 us (2%)
    psum x2, waiting for transfers between devices, body(): conv = lax.psum(partial_conv(weighted, stacked), 'tm')  170 us
    all_to_all x2, waiting for transfers between devices, body(): lax.all_to_all(sig_sites, 'mom', split_axis=0, concat_axis=2, tiled=True)  162 us
    all_to_all x1, blocking collectives, body(): lax.all_to_all(current, 'mom', split_axis=2, concat_axis=0, tiled=True)  96 us
    all_to_all x1, waiting for transfers between devices, body(): lax.all_to_all(current, 'mom', split_axis=2, concat_axis=0, tiled=True)  90.4 us
    dot_general x5, matrix products, contract(): jnp.einsum(pattern, left, right, precision=lax.Precision.HIGHEST, preferr...  81.1 us
    dot_general x8, matrix products, product(): jnp.dot(left, right, precision=lax.Precision.HIGHEST, preferred_element_t...  43.2 us
    neg x3, other arithmetic, rotated(): return jnp.concatenate([-joined[..., PANEL:], joined[..., :PANEL]], axis=-1)  21 us
    gather x4, local copies, waits for them, and re-layouts, site_sigma(): back_re = jnp.take(other_re, mirror, axis=0)  19.8 us
  transfers between devices with their start and end apart: 6, of which 6 were waited for; matrix products, arithmetic and copies ran while one was open for 4% of the time, Pallas kernels for 0%

commit v1 on v0

v1 whole, which is shorter than its diff:
```python
import functools
import math

import jax
import jax.numpy as jnp
from jax import lax
from jax.experimental import pallas as pl
from jax.experimental.pallas import tpu as pltpu
from jax.sharding import PartitionSpec as P

LSIDE = 16
K = LSIDE * LSIDE
PANEL = 64
PASSES = 2
SPIN = 2
LANES = 2 * PANEL
CHUNKS = 2
MESH = pl.DeviceIdType.MESH


def dot(left, right):
    return jnp.dot(left, right, precision=lax.Precision.HIGHEST, preferred_element_type=jnp.float32)


def dot_t(left, right):
    return lax.dot_general(
        left, right, (((1,), (1,)), ((), ())),
        precision=lax.Precision.HIGHEST, preferred_element_type=jnp.float32,
    )


def contract(pattern, left, right):
    return jnp.einsum(
        pattern, left, right, precision=lax.Precision.HIGHEST, preferred_element_type=jnp.float32
    )


def tables(ordering):
    site_index = jnp.arange(K, dtype=jnp.int32)
    site_x = site_index // LSIDE
    site_y = site_index % LSIDE
    mom_x = ordering // LSIDE
    mom_y = ordering % LSIDE
    phases = (site_x[:, None] * mom_x[None, :] + site_y[:, None] * mom_y[None, :]) % LSIDE
    angles = phases.astype(jnp.float32) * (2.0 * math.pi / LSIDE)
    return jnp.cos(angles) / LSIDE, jnp.sin(angles) / LSIDE


def rotated(joined):
    return jnp.concatenate([-joined[..., PANEL:], joined[..., :PANEL]], axis=-1)


def pass_kernel(
    n_mom, n_tm, last, cur, start, fwd_table, back_table, wvec,
    out, conv_out, recv, sig, ret, stk, part, gath,
    local_sem, fs, fr, rs, rr, ss, sr, gs, gr,
):
    mom, tm = lax.axis_index("mom"), lax.axis_index("tm")
    rows, local_k = cur.shape[3], cur.shape[4]
    share = local_k // n_tm
    step_scale = 1.0 / math.sqrt(PANEL)
    lane = lax.broadcasted_iota(jnp.int32, (1, LANES), 1)
    low = lane < PANEL
    sign = jnp.where(low, -1.0, 1.0).astype(jnp.float32)

    def swap(x):
        return pltpu.roll(x, PANEL, 1)

    def rot(x):
        return swap(x) * sign

    barrier = pltpu.get_barrier_semaphore()
    for o in range(1, n_mom):
        pl.semaphore_signal(barrier, inc=1, device_id={"mom": lax.rem(mom + o, n_mom)}, device_id_type=MESH)
    for o in range(1, n_tm):
        pl.semaphore_signal(barrier, inc=1, device_id={"tm": lax.rem(tm + o, n_tm)}, device_id_type=MESH)
    pl.semaphore_wait(barrier, n_mom + n_tm - 2)

    mine = pl.ds(mom * local_k, local_k)
    own_share = pl.ds(tm * share, share)

    def forward(c, o):
        peer = lax.rem(mom + o, n_mom)
        return pltpu.make_async_remote_copy(
            src_ref=cur.at[c, :, peer], dst_ref=recv.at[c, :, :, mine, :],
            send_sem=fs.at[c, o], recv_sem=fr.at[c, o],
            device_id={"mom": peer}, device_id_type=MESH)

    def forward_own(c):
        return pltpu.make_async_copy(cur.at[c, :, mom], recv.at[c, :, :, mine, :], local_sem.at[c])

    def back(c, o):
        peer = lax.rem(mom + o, n_mom)
        return pltpu.make_async_remote_copy(
            src_ref=sig.at[c, :, :, pl.ds(peer * local_k, local_k), :], dst_ref=ret.at[c, :, mom],
            send_sem=rs.at[c, o], recv_sem=rr.at[c, o],
            device_id={"mom": peer}, device_id_type=MESH)

    def back_own(c):
        return pltpu.make_async_copy(sig.at[c, :, :, mine, :], ret.at[c, :, mom], local_sem.at[CHUNKS + c])

    def scatter(c, o):
        peer = lax.rem(tm + o, n_tm)
        return pltpu.make_async_remote_copy(
            src_ref=part.at[c, pl.ds(peer * share, share)], dst_ref=gath.at[c, o],
            send_sem=ss.at[c, o], recv_sem=sr.at[c, o],
            device_id={"tm": peer}, device_id_type=MESH)

    def gather(c, o):
        peer = lax.rem(tm + o, n_tm)
        return pltpu.make_async_remote_copy(
            src_ref=conv_out.at[c, own_share], dst_ref=conv_out.at[c, own_share],
            send_sem=gs.at[c, o], recv_sem=gr.at[c, o],
            device_id={"tm": peer}, device_id_type=MESH)

    for c in range(CHUNKS):
        for o in range(1, n_mom):
            forward(c, o).start()
        forward_own(c).start()

    flat_cur = cur.reshape(CHUNKS * SPIN * n_mom * rows * local_k, LANES)
    flat_start = start.reshape(CHUNKS * SPIN * n_mom * rows * local_k, LANES)
    flat_ret = ret.reshape(CHUNKS * SPIN * n_mom * rows * local_k, LANES)
    group = n_mom * rows

    @pl.loop(0, local_k)
    def _(k):
        for s in range(SPIN):
            pieces = []
            for block in range(n_mom):
                for c in range(CHUNKS):
                    at = (((c * SPIN + s) * n_mom + block) * rows) * local_k + k
                    pieces.append(flat_cur[pl.ds(at, rows, stride=local_k), :])
            whole = jnp.concatenate(pieces, axis=0)
            stk[k, s, :PANEL, :] = whole
            stk[k, s, PANEL:, :] = rot(whole)

    for c in range(CHUNKS):
        for o in range(1, n_mom):
            forward(c, o).wait_recv()
        forward_own(c).wait()

        @pl.loop(0, rows)
        def _(i):
            both = jnp.concatenate([recv[c, 0, i], recv[c, 1, i]], axis=1)
            sums = dot(fwd_table[...], both)
            site, mirrored = [], []
            for s in range(SPIN):
                with_cos = sums[:K, s * LANES:(s + 1) * LANES]
                turned = rot(sums[K:, s * LANES:(s + 1) * LANES])
                site.append(with_cos + turned)
                mirrored.append(with_cos - turned)
            first, second = site
            flipped = swap(second)
            pair = (first * jnp.where(low, second, flipped)
                    + rot(first) * jnp.where(low, flipped, second)) * wvec[...]
            pair_rot = rot(pair)
            tops, bottoms = [], []
            for s in range(SPIN):
                other = mirrored[1 - s]
                flipped = swap(other)
                value = pair * jnp.where(low, other, flipped) - pair_rot * jnp.where(low, flipped, other)
                tops.append(value)
                bottoms.append(-rot(value))
            stacked = jnp.concatenate(
                [jnp.concatenate(tops, axis=1), jnp.concatenate(bottoms, axis=1)], axis=0)
            result = dot(back_table[...], stacked)
            for s in range(SPIN):
                sig[c, s, i] = result[:, s * LANES:(s + 1) * LANES]

        for o in range(1, n_mom):
            back(c, o).start()
        back_own(c).start()

    def convolve(c):
        for o in range(1, n_mom):
            back(c, o).wait_recv()
        back_own(c).wait()

        @pl.loop(0, local_k)
        def _(k):
            for s in range(SPIN):
                at = ((c * SPIN + s) * group) * local_k + k
                sigma = flat_ret[pl.ds(at, group, stride=local_k), :]
                part[c, k, s] = dot_t(sigma, stk[k, s])

        for o in range(1, n_tm):
            scatter(c, o).start()

    def reduce(c):
        for o in range(1, n_tm):
            scatter(c, o).wait_recv()

        @pl.loop(0, share)
        def _(k):
            for s in range(SPIN):
                total = part[c, tm * share + k, s]
                for o in range(1, n_tm):
                    total = total + gath[c, o, k, s]
                conv_out[c, tm * share + k, s] = total

        for o in range(1, n_tm):
            gather(c, o).start()

    def update(c):
        for o in range(1, n_tm):
            gather(c, o).wait_recv()

        @pl.loop(0, local_k)
        def _(k):
            for s in range(SPIN):
                at = ((c * SPIN + s) * group) * local_k + k
                base = flat_start[pl.ds(at, group, stride=local_k), :]
                new = base + step_scale * dot(conv_out[c, k, s], stk[k, s])
                if last:
                    for block in range(n_mom):
                        out[k, s, block, c] = new[block * rows:(block + 1) * rows, :]
                else:
                    flat_out = out.reshape(CHUNKS * SPIN * n_mom * rows * local_k, LANES)
                    flat_out[pl.ds(at, group, stride=local_k), :] = new

    for c in range(CHUNKS):
        convolve(c)
        if c > 0:
            reduce(c - 1)
    reduce(CHUNKS - 1)
    for c in range(CHUNKS):
        update(c)

    for c in range(CHUNKS):
        for o in range(1, n_mom):
            forward(c, o).wait_send()
            back(c, o).wait_send()
        for o in range(1, n_tm):
            scatter(c, o).wait_send()
            gather(c, o).wait_send()


def corrector(n_mom, n_tm, last, cur, start, fwd_table, back_table, wvec):
    rows, local_k = cur.shape[3], cur.shape[4]
    panel = (CHUNKS, SPIN, n_mom, rows, local_k, LANES)
    conv = (CHUNKS, local_k, SPIN, n_mom * rows, LANES)
    out_shape = (local_k, SPIN, n_mom, CHUNKS, rows, LANES) if last else panel
    dma = pltpu.SemaphoreType.DMA
    vmem = pl.BlockSpec(memory_space=pltpu.VMEM)
    return pl.pallas_call(
        functools.partial(pass_kernel, n_mom, n_tm, last),
        out_shape=(jax.ShapeDtypeStruct(out_shape, jnp.float32), jax.ShapeDtypeStruct(conv, jnp.float32)),
        in_specs=[vmem] * 5,
        out_specs=(vmem, vmem),
        scratch_shapes=[
            pltpu.VMEM((CHUNKS, SPIN, rows, K, LANES), jnp.float32),
            pltpu.VMEM((CHUNKS, SPIN, rows, K, LANES), jnp.float32),
            pltpu.VMEM(panel, jnp.float32),
            pltpu.VMEM((local_k, SPIN, LANES, LANES), jnp.float32),
            pltpu.VMEM(conv, jnp.float32),
            pltpu.VMEM((CHUNKS, n_tm, local_k // n_tm, SPIN, n_mom * rows, LANES), jnp.float32),
            dma((2 * CHUNKS,)),
            dma((CHUNKS, n_mom)), dma((CHUNKS, n_mom)),
            dma((CHUNKS, n_mom)), dma((CHUNKS, n_mom)),
            dma((CHUNKS, n_tm)), dma((CHUNKS, n_tm)),
            dma((CHUNKS, n_tm)), dma((CHUNKS, n_tm)),
        ],
        compiler_params=pltpu.CompilerParams(
            collective_id=1 if last else 0, has_side_effects=True, vmem_limit_bytes=60 * 1024 * 1024),
        name="last_pass" if last else "first_pass",
    )(cur, start, fwd_table, back_table, wvec)


def own_block(guess, conv, step_scale):
    stacked = jnp.concatenate([conv, rotated(conv)], axis=2)
    return guess + step_scale * contract("ksab,ksbc->ksac", guess, stacked)


def body(panel_start, block_guess, coupling, slab_owner, expiring, ordering):
    slab_count = lax.axis_size("tm")
    n_mom = lax.axis_size("mom")
    own_index = lax.axis_index("tm")
    cos_table, sin_table = tables(ordering)
    fwd_table = jnp.concatenate([cos_table, sin_table], axis=0)
    back_table = fwd_table.T
    back_table = jnp.concatenate([cos_table.T, sin_table.T], axis=1)
    blocks = jnp.arange(slab_count, dtype=jnp.int32)
    slab_mine = jnp.sum(blocks * (slab_owner == own_index).astype(jnp.int32))
    position = (slab_mine - expiring[0]) % slab_count
    window = slab_count * PANEL
    times = position * PANEL + jnp.arange(PANEL, dtype=jnp.int32)
    weights = jnp.exp(-1.5 * (window - 1 - times).astype(jnp.float32) / window) / math.sqrt(window)
    strength = coupling[0] * coupling[0]
    wvec = (strength * jnp.concatenate([weights, weights]))[None, :]
    step_scale = 1.0 / math.sqrt(PANEL)
    guess_full = lax.all_gather(block_guess, "tm", axis=2, tiled=True)

    local_k = panel_start.shape[0]
    rows = PANEL // (n_mom * CHUNKS)
    start = panel_start.reshape(local_k, SPIN, n_mom, CHUNKS, rows, LANES).transpose(3, 1, 2, 4, 0, 5)
    current = start
    for sweep in range(PASSES):
        current, conv = corrector(
            n_mom, slab_count, sweep == PASSES - 1, current, start, fwd_table, back_table, wvec)
    current = current.reshape(panel_start.shape)
    conv = conv.reshape(CHUNKS, local_k, SPIN, n_mom, rows, LANES).transpose(1, 2, 3, 0, 4, 5)
    block = own_block(guess_full, conv.reshape(panel_start.shape), step_scale)
    owner_expiring = jnp.sum(slab_owner * (blocks == expiring[0]).astype(jnp.int32))
    return jnp.where(own_index == owner_expiring, block, current)


def solution(mesh):
    return jax.shard_map(
        body,
        mesh=mesh,
        in_specs=(
            P("mom", "groups", None, "tm"),
            P("mom", "groups", "tm", None),
            P("groups"),
            P("groups"),
            P("groups"),
            P(),
        ),
        out_specs=P("mom", "groups", None, "tm"),
        check_vma=False,
    )
```

time: 887 us -> 655 us (0.74)
  the two profiles are of different devices: /device:TPU:26 before, /device:TPU:23 now
where the time goes in v1:
time: 655 us
  Pallas kernels  598 us (91%)
  matrix products  18.3 us (3%)
  between operations  16 us (2%)
  local copies, waits for them, and re-layouts  11.1 us (2%)
  other arithmetic  10.5 us (2%)
    pallas_call x2, Pallas kernels, corrector(): pl.pallas_call(functools.partial(pass_kernel, n_mom, n_tm, last), out_sha...  598 us
    dot_general x1, matrix products, contract(): jnp.einsum(pattern, left, right, precision=lax.Precision.HIGHEST, preferr...  18.3 us
  transfers between devices with their start and end apart: 1, of which 0 were waited for; matrix products, arithmetic and copies ran while one was open for 3% of the time, Pallas kernels for 91%

profile of v1, /device:TPU:23, one launch (start us, length us, event | category | flops | bytes accessed | tf_op | source)
XLA Modules:
  0.0 654.6 jit_solution(9761836009362154662)
XLA Ops:
  6.5 0.0 all-gather.2.cloned.1.call-start
  6.5 0.7 all-gather.2.cloned.1.call-update
  7.9 1.3 fusion.16
  11.1 0.0 copy-start.1
  11.1 6.6 %copy.11 = f32[64,2,4,2,8,128]{5,0,4,2,1,3:T(8,128)} copy(f32[64,2,4,2,8,128]{5,4,3,2,1,0:T(8,128)} %bitcast.26) | data formatting | bytes 8388608 | tf_op jit(solution)/shard_map/reshape | solution.py:296
  17.8 0.6 maximum_multiply_fusion.wvec
  18.4 0.0 copy-done.1
  18.4 2.2 cosine_multiply_fusion
  20.6 0.9 pad_maximum_fusion.1.back_table
  21.5 0.8 pad_maximum_fusion.fwd_table
  22.3 284.7 %first_pass.1 = (f32[2,2,4,8,64,128]{5,4,3,2,1,0:T(8,128)}, f32[2,64,2,32,128]{4,3,2,1,0:T(8,128)}) custom-call(f32[2,2,4,8,64,128]{5,4,3,2,1,0:T(8,128)} %bitcast.21, f32[2,2,4,8,64,128]{5,4,3,2,1,0:T(8,128)} %bitcast.22, f32[512,256]{1,0:T(8,128)} %pad_maximum_fusion.fwd_table, f32[256,512]{1,0:T(8,128)} %pad_maximum_fusion.1.back_table, ...), custom_call_target="tpu_custom_call" | custom-call | tf_op jit(solution)/shard_map/first_pass/pallas_call | solution.py:246
  307.0 313.3 %last_pass.1 = (f32[64,2,4,2,8,128]{5,4,3,2,1,0:T(8,128)}, f32[2,64,2,32,128]{4,3,2,1,0:T(8,128)}) custom-call(f32[2,2,4,8,64,128]{5,4,3,2,1,0:T(8,128)} %get-tuple-element.8.cur, f32[2,2,4,8,64,128]{5,4,3,2,1,0:T(8,128)} %bitcast.23, f32[512,256]{1,0:T(8,128)} %pad_maximum_fusion.fwd_table, f32[256,512]{1,0:T(8,128)} %pad_maximum_fusion.1.back_table, ...), custom_call_target="tpu_custom_call" | custom-call | tf_op jit(solution)/shard_map/last_pass/pallas_call | solution.py:246
  620.4 2.6 copy.9
  622.9 0.0 copy-start
  623.0 1.9 copy-done
  624.9 4.6 slice_negate_fusion
  629.5 0.0 all-gather.2.cloned.1.call-done
  629.5 18.3 %bitcast_select_fusion = f32[64,2,64,128]{3,2,1,0:T(8,128)} fusion(f32[64,2,4,2,8,128]{5,4,3,2,1,0:T(8,128)} %get-tuple-element.10, f32[64,2,64,128]{3,2,1,0:T(8,128)} %all-gather.2.cloned.1.call-done, pred[]{:T(512)S(6)} %eq.24, f32[64,2,64,64]{3,2,1,0:T(8,128)} %get-tuple-element.14, f32[64,2,64,64]{3,2,1,0:T(8,128)} %get-tuple-element.13, ...), kind=kOutput, calls=%fused_computation.7 | convolution fusion | flops 1617952768 | bytes 20971520 | tf_op jit(solution)/shard_map/ksab,ksbc->ksac/dot_general | solution.py:33
  (3 shorter events, 0.0 us)
Async XLA Ops:
  6.5 623.0 %all-gather.2.cloned.1.call-start = ((), (), s32[]{:S(2)}) async-start(), calls=%async_computation | async-start | bytes 5242880 | tf_op jit(solution)/shard_map/all_gather | solution.py:292
  11.1 7.3 %copy-start.1 = (s32[256]{0:T(256)S(1)}, s32[256]{0:T(256)}, u32[]{:S(2)}) copy-start(s32[256]{0:T(256)} %param.11) | copy-start | bytes 3076
  622.9 1.9 copy-start
Sparse Core Ops, SparseCore 0:
  8.9 34.9 all-gather.1

commit v2 on v0

v2 whole, which is shorter than its diff:
```python
import functools
import math

import jax
import jax.numpy as jnp
from jax import lax
from jax.experimental import pallas as pl
from jax.experimental.pallas import tpu as pltpu
from jax.sharding import PartitionSpec as P

LSIDE = 16
K = LSIDE * LSIDE
PANEL = 64
PASSES = 2
SPIN = 2
LANES = 2 * PANEL
CHUNKS = 2
MESH = pl.DeviceIdType.MESH


def tables(ordering):
    site_index = jnp.arange(K, dtype=jnp.int32)
    site_x = site_index // LSIDE
    site_y = site_index % LSIDE
    mom_x = ordering // LSIDE
    mom_y = ordering % LSIDE
    phases = (site_x[:, None] * mom_x[None, :] + site_y[:, None] * mom_y[None, :]) % LSIDE
    angles = phases.astype(jnp.float32) * (2.0 * math.pi / LSIDE)
    return jnp.cos(angles) / LSIDE, jnp.sin(angles) / LSIDE


def split(x):
    high = x.astype(jnp.bfloat16)
    return high, (x - high.astype(jnp.float32)).astype(jnp.bfloat16)


def dot3(left, right, transposed=False):
    dims = (((1,), (1 if transposed else 0,)), ((), ()))

    def one(a, b):
        return lax.dot_general(a, b, dims, preferred_element_type=jnp.float32)

    return one(left[0], right[0]) + (one(left[0], right[1]) + one(left[1], right[0]))


def step_kernel(
    n_mom, n_tm, start, guess, fwd_table, back_table, wvec, chosen,
    out, cur, recv, sig, ret, fwd_split, back_split, stk, part, conv, pair_buf, ring_buf, guess_all,
    local_sem, guess_own, fs, fr, rs, rr, ps, pr, ss, sr, gs, gr, qs, qr, ds, dr,
):
    mom, tm = lax.axis_index("mom"), lax.axis_index("tm")
    rows, local_k = cur.shape[3], cur.shape[4]
    group = n_mom * rows
    n_x = n_tm // 2
    half = local_k // 2
    share = half // n_x
    tm_x, core = tm // 2, tm % 2
    step_scale = 1.0 / math.sqrt(PANEL)
    lane = lax.broadcasted_iota(jnp.int32, (1, LANES), 1)
    low = lane < PANEL
    sign = jnp.where(low, -1.0, 1.0).astype(jnp.float32)
    flat_cur = cur.reshape(CHUNKS * SPIN * group * local_k, LANES)
    flat_ret = ret.reshape(CHUNKS * SPIN * group * local_k, LANES)

    def swap(x):
        return pltpu.roll(x, PANEL, 1)

    def rot(x):
        return swap(x) * sign

    barrier = pltpu.get_barrier_semaphore()
    for o in range(1, n_mom):
        pl.semaphore_signal(barrier, inc=1, device_id={"mom": lax.rem(mom + o, n_mom)}, device_id_type=MESH)
    for o in range(1, n_tm):
        pl.semaphore_signal(barrier, inc=1, device_id={"tm": lax.rem(tm + o, n_tm)}, device_id_type=MESH)

    mine = pl.ds(mom * local_k, local_k)
    own_half = pl.ds(core * half, half)
    other_half = pl.ds((1 - core) * half, half)
    share_at = core * half + tm_x * share
    own_share = pl.ds(share_at, share)
    partner = {"tm": tm_x * 2 + (1 - core)}

    def remote(source, target, send, recv_sem, device):
        return pltpu.make_async_remote_copy(
            src_ref=source, dst_ref=target, send_sem=send, recv_sem=recv_sem,
            device_id=device, device_id_type=MESH)

    def forward(n, c, o):
        peer = lax.rem(mom + o, n_mom)
        return remote(cur.at[c, :, peer], recv.at[c, :, :, mine, :], fs.at[n, c, o], fr.at[n, c, o], {"mom": peer})

    def forward_own(n, c):
        return pltpu.make_async_copy(cur.at[c, :, mom], recv.at[c, :, :, mine, :], local_sem.at[n, c, 0])

    def back(n, c, o):
        peer = lax.rem(mom + o, n_mom)
        return remote(
            sig.at[c, :, :, pl.ds(peer * local_k, local_k), :], ret.at[c, :, mom],
            rs.at[n, c, o], rr.at[n, c, o], {"mom": peer})

    def back_own(n, c):
        return pltpu.make_async_copy(sig.at[c, :, :, mine, :], ret.at[c, :, mom], local_sem.at[n, c, 1])

    def pair_up(n, c):
        return remote(part.at[c, other_half], pair_buf.at[c], ps.at[n, c], pr.at[n, c], partner)

    def scatter(n, c, o):
        peer = lax.rem(tm_x + o, n_x)
        return remote(
            part.at[c, pl.ds(core * half + peer * share, share)], ring_buf.at[c, o - 1],
            ss.at[n, c, o], sr.at[n, c, o], {"tm": peer * 2 + core})

    def gather(n, c, o):
        peer = lax.rem(tm_x + o, n_x)
        return remote(
            conv.at[c, own_share], conv.at[c, own_share],
            gs.at[n, c, o], gr.at[n, c, o], {"tm": peer * 2 + core})

    def pair_down(n, c):
        return remote(conv.at[c, own_half], conv.at[c, own_half], qs.at[n, c], qr.at[n, c], partner)

    def guess_copy(o):
        return remote(guess, guess_all.at[tm], ds.at[o], dr.at[o], {"tm": lax.rem(tm + o, n_tm)})

    def guess_local():
        return pltpu.make_async_copy(guess, guess_all.at[tm], guess_own)

    def send_forward(n, c):
        for o in range(1, n_mom):
            forward(n, c, o).start()
        forward_own(n, c).start()

    def keep_stack(n, k, s, c, value):
        turned = rot(value)
        for at, piece in ((c * group, value), (PANEL + c * group, turned)):
            high, rest = split(piece)
            stk[n, 0, k, s, at:at + group, :] = high
            stk[n, 1, k, s, at:at + group, :] = rest

    def first_layout(c):
        @pl.loop(0, local_k)
        def _(k):
            for s in range(SPIN):
                at = ((c * SPIN + s) * group) * local_k + k
                flat_cur[pl.ds(at, group, stride=local_k), :] = start[k, s, c]

    def sigma(n, c):
        for o in range(1, n_mom):
            forward(n, c, o).wait_recv()
        forward_own(n, c).wait()
        if n > 0:
            for o in range(1, n_mom):
                back(n - 1, c, o).wait_send()

        @pl.loop(0, rows)
        def _(i):
            both = jnp.concatenate([recv[c, 0, i], recv[c, 1, i]], axis=1)
            sums = dot3((fwd_split[0], fwd_split[1]), split(both))
            site, mirrored = [], []
            for s in range(SPIN):
                with_cos = sums[:K, s * LANES:(s + 1) * LANES]
                turned = rot(sums[K:, s * LANES:(s + 1) * LANES])
                site.append(with_cos + turned)
                mirrored.append(with_cos - turned)
            first, second = site
            flipped = swap(second)
            pair = (first * jnp.where(low, second, flipped)
                    + rot(first) * jnp.where(low, flipped, second)) * wvec[...]
            pair_rot = rot(pair)
            tops, bottoms = [], []
            for s in range(SPIN):
                other = mirrored[1 - s]
                flipped = swap(other)
                value = pair * jnp.where(low, other, flipped) - pair_rot * jnp.where(low, flipped, other)
                tops.append(value)
                bottoms.append(-rot(value))
            stacked = jnp.concatenate(
                [jnp.concatenate(tops, axis=1), jnp.concatenate(bottoms, axis=1)], axis=0)
            result = dot3((back_split[0], back_split[1]), split(stacked))
            for s in range(SPIN):
                sig[c, s, i] = result[:, s * LANES:(s + 1) * LANES]

        for o in range(1, n_mom):
            back(n, c, o).start()
        back_own(n, c).start()

    def convolve(n, c):
        for o in range(1, n_mom):
            back(n, c, o).wait_recv()
        back_own(n, c).wait()
        if n > 0:
            pair_up(n - 1, c).wait_send()
            pair_down(n - 1, c).wait_send()
            for o in range(1, n_x):
                scatter(n - 1, c, o).wait_send()
                gather(n - 1, c, o).wait_send()

        def some(base):
            @pl.loop(0, half, unroll=2)
            def _(i):
                k = base + i
                for s in range(SPIN):
                    at = ((c * SPIN + s) * group) * local_k + k
                    value = split(flat_ret[pl.ds(at, group, stride=local_k), :])
                    part[c, k, s] = dot3(value, (stk[n, 0, k, s], stk[n, 1, k, s]), True)

        some((1 - core) * half)
        pair_up(n, c).start()
        some(core * half)

    def reduce(n, c):
        pair_up(n, c).wait_recv()

        @pl.loop(0, half)
        def _(i):
            part[c, core * half + i] = part[c, core * half + i] + pair_buf[c, i]

        for o in range(1, n_x):
            scatter(n, c, o).start()
        for o in range(1, n_x):
            scatter(n, c, o).wait_recv()

        @pl.loop(0, share)
        def _(i):
            total = part[c, share_at + i]
            for o in range(1, n_x):
                total = total + ring_buf[c, o - 1, i]
            conv[c, share_at + i] = total

        for o in range(1, n_x):
            gather(n, c, o).start()
        for o in range(1, n_x):
            gather(n, c, o).wait_recv()
        pair_down(n, c).start()

    def update(n, c):
        last = n == PASSES - 1
        if not last:
            for o in range(1, n_mom):
                forward(n, c, o).wait_send()

        def some(base):
            @pl.loop(0, half, unroll=2)
            def _(i):
                k = base + i
                for s in range(SPIN):
                    new = start[k, s, c] + step_scale * dot3(
                        split(conv[c, k, s]), (stk[n, 0, k, s], stk[n, 1, k, s]))
                    if last:
                        out[k, s, c] = new
                    else:
                        at = ((c * SPIN + s) * group) * local_k + k
                        flat_cur[pl.ds(at, group, stride=local_k), :] = new
                        keep_stack(n + 1, k, s, c, new)

        some(core * half)
        pair_down(n, c).wait_recv()
        some((1 - core) * half)

    first_layout(0)
    pl.semaphore_wait(barrier, n_mom + n_tm - 2)
    send_forward(0, 0)
    for c in range(1, CHUNKS):
        first_layout(c)
        send_forward(0, c)
    for o in range(1, n_tm):
        guess_copy(o).start()
    guess_local().start()

    fwd_split[0], fwd_split[1] = split(fwd_table[...])
    back_split[0], back_split[1] = split(back_table[...])

    @pl.loop(0, local_k)
    def _(k):
        for s in range(SPIN):
            for c in range(CHUNKS):
                keep_stack(0, k, s, c, start[k, s, c])

    for n in range(PASSES):
        for c in range(CHUNKS):
            sigma(n, c)
        for c in range(CHUNKS):
            convolve(n, c)
            reduce(n, c)
            update(n, c)
            if n < PASSES - 1:
                send_forward(n + 1, c)

    for o in range(1, n_tm):
        guess_copy(o).wait_recv()
    guess_local().wait()

    @pl.loop(0, local_k)
    def _(k):
        for s in range(SPIN):
            d = jnp.concatenate([guess_all[t, k, s] for t in range(n_tm)], axis=0)
            whole = jnp.concatenate([conv[c, k, s] for c in range(CHUNKS)], axis=0)
            stacked = jnp.concatenate([whole, rot(whole)], axis=0)
            block = d + step_scale * dot3(split(d), split(stacked))
            for c in range(CHUNKS):
                out[k, s, c] = jnp.where(
                    chosen[...] > 0.5, block[c * group:(c + 1) * group, :], out[k, s, c])

    n = PASSES - 1
    for c in range(CHUNKS):
        pair_up(n, c).wait_send()
        pair_down(n, c).wait_send()
        for o in range(1, n_x):
            scatter(n, c, o).wait_send()
            gather(n, c, o).wait_send()
        for o in range(1, n_mom):
            forward(n, c, o).wait_send()
            back(n, c, o).wait_send()
    for o in range(1, n_tm):
        guess_copy(o).wait_send()


def panel_step(n_mom, n_tm, start, guess, fwd_table, back_table, wvec, chosen):
    local_k = start.shape[0]
    group = start.shape[3]
    rows = group // n_mom
    share = local_k // n_tm
    panel = (CHUNKS, SPIN, n_mom, rows, local_k, LANES)
    sites = (CHUNKS, SPIN, rows, K, LANES)
    f32, bf16 = jnp.float32, jnp.bfloat16
    dma = pltpu.SemaphoreType.DMA
    vmem = pl.BlockSpec(memory_space=pltpu.VMEM)
    one, many_mom, many_x = (PASSES, CHUNKS), (PASSES, CHUNKS, n_mom), (PASSES, CHUNKS, n_tm // 2)
    return pl.pallas_call(
        functools.partial(step_kernel, n_mom, n_tm),
        out_shape=jax.ShapeDtypeStruct(start.shape, f32),
        in_specs=[vmem] * 6,
        out_specs=vmem,
        scratch_shapes=[
            pltpu.VMEM(panel, f32),
            pltpu.VMEM(sites, f32),
            pltpu.VMEM(sites, f32),
            pltpu.VMEM(panel, f32),
            pltpu.VMEM((2, 2 * K, K), bf16),
            pltpu.VMEM((2, K, 2 * K), bf16),
            pltpu.VMEM((PASSES, 2, local_k, SPIN, LANES, LANES), bf16),
            pltpu.VMEM((CHUNKS, local_k, SPIN, group, LANES), f32),
            pltpu.VMEM((CHUNKS, local_k, SPIN, group, LANES), f32),
            pltpu.VMEM((CHUNKS, local_k // 2, SPIN, group, LANES), f32),
            pltpu.VMEM((CHUNKS, max(n_tm // 2 - 1, 1), share, SPIN, group, LANES), f32),
            pltpu.VMEM((n_tm,) + guess.shape, f32),
            dma(one + (2,)), dma,
            dma(many_mom), dma(many_mom), dma(many_mom), dma(many_mom),
            dma(one), dma(one),
            dma(many_x), dma(many_x), dma(many_x), dma(many_x),
            dma(one), dma(one),
            dma((n_tm,)), dma((n_tm,)),
        ],
        compiler_params=pltpu.CompilerParams(
            collective_id=0, has_side_effects=True, vmem_limit_bytes=63 * 1024 * 1024),
        name="panel_step",
    )(start, guess, fwd_table, back_table, wvec, chosen)


def body(panel_start, block_guess, coupling, slab_owner, expiring, ordering):
    slab_count = lax.axis_size("tm")
    n_mom = lax.axis_size("mom")
    own_index = lax.axis_index("tm")
    cos_table, sin_table = tables(ordering)
    fwd_table = jnp.concatenate([cos_table, sin_table], axis=0)
    back_table = jnp.concatenate([cos_table.T, sin_table.T], axis=1)
    blocks = jnp.arange(slab_count, dtype=jnp.int32)
    slab_mine = jnp.sum(blocks * (slab_owner == own_index).astype(jnp.int32))
    position = (slab_mine - expiring[0]) % slab_count
    window = slab_count * PANEL
    times = position * PANEL + jnp.arange(PANEL, dtype=jnp.int32)
    weights = jnp.exp(-1.5 * (window - 1 - times).astype(jnp.float32) / window) / math.sqrt(window)
    strength = coupling[0] * coupling[0]
    wvec = (strength * jnp.concatenate([weights, weights]))[None, :]
    owner_expiring = jnp.sum(slab_owner * (blocks == expiring[0]).astype(jnp.int32))
    chosen = jnp.broadcast_to((own_index == owner_expiring).astype(jnp.float32), (1, LANES))
    local_k = panel_start.shape[0]
    start = panel_start.reshape(local_k, SPIN, CHUNKS, PANEL // CHUNKS, LANES)
    result = panel_step(n_mom, slab_count, start, block_guess, fwd_table, back_table, wvec, chosen)
    return result.reshape(panel_start.shape)


def solution(mesh):
    return jax.shard_map(
        body,
        mesh=mesh,
        in_specs=(
            P("mom", "groups", None, "tm"),
            P("mom", "groups", "tm", None),
            P("groups"),
            P("groups"),
            P("groups"),
            P(),
        ),
        out_specs=P("mom", "groups", None, "tm"),
        check_vma=False,
    )
```

time: 887 us -> 461 us (0.52)
  Pallas kernels: 0 us -> 446 us
  waiting for transfers between devices: 441 us -> 0 us
  local copies, waits for them, and re-layouts: 136 us -> 5.37 us
  matrix products: 124 us -> 0 us
  blocking collectives: 96 us -> 0 us
  other arithmetic: 43.8 us -> 6.46 us
  starting transfers between devices: 19.6 us -> 0 us
  between operations: 16.5 us -> 2.54 us
    pallas_call x0 -> x1, Pallas kernels: none -> 446 us  [panel_step(): pl.pallas_call(functools.partial(step_kernel, n_mom, n_tm), out_shape=jax...]
    all_to_all x3 -> x0, waiting for transfers between devices: 252 us -> none  [the longest x2 162 us: body(): lax.all_to_all(sig_sites, 'mom', split_axis=0, concat_axis=2, tiled=True)]
    psum x2 -> x0, waiting for transfers between devices: 170 us -> none  [body(): conv = lax.psum(partial_conv(weighted, stacked), 'tm')]
    dot_general x13 -> x0, matrix products: 124 us -> none  [the longest x5 81.1 us: contract(): jnp.einsum(pattern, left, right, precision=lax.Precision.HIGHEST, preferr...]
    all_to_all x1 -> x0, blocking collectives: 96 us -> none  [body(): lax.all_to_all(current, 'mom', split_axis=2, concat_axis=0, tiled=True)]
    gather x8 -> x0, local copies, waits for them, and re-layouts: 38.9 us -> none  [the longest x4 19.8 us: site_sigma(): back_re = jnp.take(other_re, mirror, axis=0)]
    rev x8 -> x0, local copies, waits for them, and re-layouts: 31.5 us -> none  [the longest x4 17.4 us: site_sigma(): other_im = site_im[:, ::-1]]
    neg x3 -> x0, other arithmetic: 21 us -> none  [rotated(): return jnp.concatenate([-joined[..., PANEL:], joined[..., :PANEL]], axis=-1)]
  transfers between devices with their start and end apart: 6 -> 0, of which waited for: 6 -> 0; matrix products, arithmetic and copies ran while one was open for 4% -> 0% of each run, Pallas kernels for 0% -> 0%
where the time goes in v2:
time: 461 us; the launch traced here: 460 us
  Pallas kernels  446 us (97%)
  other arithmetic  6.46 us (1%)
  local copies, waits for them, and re-layouts  5.37 us (1%)
    pallas_call x1, Pallas kernels, panel_step(): pl.pallas_call(functools.partial(step_kernel, n_mom, n_tm), out_shape=jax...  446 us

profile of v2, /device:TPU:26, one launch (start us, length us, event | category | flops | bytes accessed | tf_op | source)
XLA Modules:
  0.0 460.5 jit_solution(2019636644396587652)
XLA Ops:
  1.3 1.3 fusion.9
  3.9 0.6 broadcast_in_dim.2.chosen
  4.4 0.6 maximum_multiply_fusion.wvec
  5.0 0.7 and_select_fusion.2
  5.7 2.2 cosine_multiply_fusion
  7.9 0.9 pad_maximum_fusion.1.back_table
  8.7 0.8 pad_maximum_fusion.fwd_table
  9.6 446.1 %panel_step.1 = f32[64,2,2,32,128]{4,3,2,1,0:T(8,128)} custom-call(f32[64,2,2,32,128]{4,3,2,1,0:T(8,128)} %bitcast.9, f32[64,2,16,128]{3,2,1,0:T(8,128)} %guess.1, f32[512,256]{1,0:T(8,128)} %pad_maximum_fusion.fwd_table, f32[256,512]{1,0:T(8,128)} %pad_maximum_fusion.1.back_table, f32[1,128]{1,0:T(1,128)} %maximum_multiply_fusion.wvec, ...), custom_call_target="tpu_custom_call" | custom-call | tf_op jit(solution)/shard_map/panel_step/pallas_call | solution.py:330
  455.7 4.8 %copy.10 = f32[64,2,64,128]{3,2,1,0:T(8,128)} copy(f32[64,2,64,128]{3,2,1,0:T(8,128)} %bitcast.8) | data formatting | bytes 8388608
  (2 shorter events, 0.0 us)

commit v3 on v2

--- a/solution.py
+++ b/solution.py
@@ -197,7 +197,7 @@
                 gather(n - 1, c, o).wait_send()
 
         def some(base):
-            @pl.loop(0, half, unroll=2)
+            @pl.loop(0, half, unroll=8)
             def _(i):
                 k = base + i
                 for s in range(SPIN):
@@ -235,27 +235,46 @@
         pair_down(n, c).start()
 
     def update(n, c):
-        last = n == PASSES - 1
-        if not last:
-            for o in range(1, n_mom):
-                forward(n, c, o).wait_send()
+        for o in range(1, n_mom):
+            forward(n, c, o).wait_send()
 
         def some(base):
-            @pl.loop(0, half, unroll=2)
+            @pl.loop(0, half, unroll=8)
             def _(i):
                 k = base + i
                 for s in range(SPIN):
                     new = start[k, s, c] + step_scale * dot3(
                         split(conv[c, k, s]), (stk[n, 0, k, s], stk[n, 1, k, s]))
-                    if last:
-                        out[k, s, c] = new
-                    else:
-                        at = ((c * SPIN + s) * group) * local_k + k
-                        flat_cur[pl.ds(at, group, stride=local_k), :] = new
-                        keep_stack(n + 1, k, s, c, new)
+                    at = ((c * SPIN + s) * group) * local_k + k
+                    flat_cur[pl.ds(at, group, stride=local_k), :] = new
+                    keep_stack(n + 1, k, s, c, new)
 
         some(core * half)
         pair_down(n, c).wait_recv()
+        some((1 - core) * half)
+
+    def finish(n):
+        is_block = chosen[...] > 0.5
+
+        def some(base):
+            @pl.loop(0, half, unroll=4)
+            def _(i):
+                k = base + i
+                for s in range(SPIN):
+                    whole = jnp.concatenate([conv[c, k, s] for c in range(CHUNKS)], axis=0)
+                    d = jnp.concatenate([guess_all[t, k, s] for t in range(n_tm)], axis=0)
+                    first = jnp.concatenate([start[k, s, c] for c in range(CHUNKS)], axis=0)
+                    panel = stk[n, 0, k, s].astype(jnp.float32) + stk[n, 1, k, s].astype(jnp.float32)
+                    right = jnp.where(is_block, jnp.concatenate([whole, rot(whole)], axis=0), panel)
+                    left = jnp.where(is_block, d, whole)
+                    new = jnp.where(is_block, d, first) + step_scale * dot3(split(left), split(right))
+                    for c in range(CHUNKS):
+                        out[k, s, c] = new[c * group:(c + 1) * group, :]
+
+        for c in range(CHUNKS - 1):
+            pair_down(n, c).wait_recv()
+        some(core * half)
+        pair_down(n, CHUNKS - 1).wait_recv()
         some((1 - core) * half)
 
     first_layout(0)
@@ -271,7 +290,7 @@
     fwd_split[0], fwd_split[1] = split(fwd_table[...])
     back_split[0], back_split[1] = split(back_table[...])
 
-    @pl.loop(0, local_k)
+    @pl.loop(0, local_k, unroll=4)
     def _(k):
         for s in range(SPIN):
             for c in range(CHUNKS):
@@ -283,24 +302,14 @@
         for c in range(CHUNKS):
             convolve(n, c)
             reduce(n, c)
-            update(n, c)
             if n < PASSES - 1:
+                update(n, c)
                 send_forward(n + 1, c)
 
     for o in range(1, n_tm):
         guess_copy(o).wait_recv()
     guess_local().wait()
-
-    @pl.loop(0, local_k)
-    def _(k):
-        for s in range(SPIN):
-            d = jnp.concatenate([guess_all[t, k, s] for t in range(n_tm)], axis=0)
-            whole = jnp.concatenate([conv[c, k, s] for c in range(CHUNKS)], axis=0)
-            stacked = jnp.concatenate([whole, rot(whole)], axis=0)
-            block = d + step_scale * dot3(split(d), split(stacked))
-            for c in range(CHUNKS):
-                out[k, s, c] = jnp.where(
-                    chosen[...] > 0.5, block[c * group:(c + 1) * group, :], out[k, s, c])
+    finish(PASSES - 1)
 
     n = PASSES - 1
     for c in range(CHUNKS):

time: 461 us -> 432 us (0.937)
  Pallas kernels: 446 us -> 417 us
    pallas_call x1, Pallas kernels: 446 us -> 417 us  [panel_step(): pl.pallas_call(functools.partial(step_kernel, n_mom, n_tm), out_shape=jax...]
where the time goes in v3:
time: 432 us; the launch traced here: 431 us
  Pallas kernels  417 us (97%)
  other arithmetic  6.46 us (1%)
  local copies, waits for them, and re-layouts  5.37 us (1%)
    pallas_call x1, Pallas kernels, panel_step(): pl.pallas_call(functools.partial(step_kernel, n_mom, n_tm), out_shape=jax...  417 us

profile of v3, /device:TPU:26, one launch (start us, length us, event | category | flops | bytes accessed | tf_op | source)
XLA Modules:
  0.0 431.3 jit_solution(5720159226216715168)
XLA Ops:
  1.3 1.3 fusion.9
  3.9 0.6 broadcast_in_dim.2.chosen
  4.4 0.6 maximum_multiply_fusion.wvec
  5.0 0.7 and_select_fusion.2
  5.7 2.2 cosine_multiply_fusion
  7.9 0.9 pad_maximum_fusion.1.back_table
  8.7 0.8 pad_maximum_fusion.fwd_table
  9.6 417.0 %panel_step.1 = f32[64,2,2,32,128]{4,3,2,1,0:T(8,128)} custom-call(f32[64,2,2,32,128]{4,3,2,1,0:T(8,128)} %bitcast.9, f32[64,2,16,128]{3,2,1,0:T(8,128)} %guess.1, f32[512,256]{1,0:T(8,128)} %pad_maximum_fusion.fwd_table, f32[256,512]{1,0:T(8,128)} %pad_maximum_fusion.1.back_table, f32[1,128]{1,0:T(1,128)} %maximum_multiply_fusion.wvec, ...), custom_call_target="tpu_custom_call" | custom-call | tf_op jit(solution)/shard_map/panel_step/pallas_call | solution.py:339
  426.5 4.8 %copy.10 = f32[64,2,64,128]{3,2,1,0:T(8,128)} copy(f32[64,2,64,128]{3,2,1,0:T(8,128)} %bitcast.8) | data formatting | bytes 8388608
  (2 shorter events, 0.0 us)

commit v4 on v3

--- a/solution.py
+++ b/solution.py
@@ -19,12 +19,9 @@
 
 
 def tables(ordering):
-    site_index = jnp.arange(K, dtype=jnp.int32)
-    site_x = site_index // LSIDE
-    site_y = site_index % LSIDE
-    mom_x = ordering // LSIDE
-    mom_y = ordering % LSIDE
-    phases = (site_x[:, None] * mom_x[None, :] + site_y[:, None] * mom_y[None, :]) % LSIDE
+    bits = LSIDE.bit_length() - 1
+    site = lax.broadcasted_iota(jnp.int32, (K, K), 0)
+    phases = ((site >> bits) * (ordering >> bits) + (site & (LSIDE - 1)) * (ordering & (LSIDE - 1))) & (LSIDE - 1)
     angles = phases.astype(jnp.float32) * (2.0 * math.pi / LSIDE)
     return jnp.cos(angles) / LSIDE, jnp.sin(angles) / LSIDE
 
@@ -44,7 +41,7 @@
 
 
 def step_kernel(
-    n_mom, n_tm, start, guess, fwd_table, back_table, wvec, chosen,
+    n_mom, n_tm, start, guess, ordering, wvec, chosen,
     out, cur, recv, sig, ret, fwd_split, back_split, stk, part, conv, pair_buf, ring_buf, guess_all,
     local_sem, guess_own, fs, fr, rs, rr, ps, pr, ss, sr, gs, gr, qs, qr, ds, dr,
 ):
@@ -75,7 +72,6 @@
         pl.semaphore_signal(barrier, inc=1, device_id={"tm": lax.rem(tm + o, n_tm)}, device_id_type=MESH)
 
     mine = pl.ds(mom * local_k, local_k)
-    own_half = pl.ds(core * half, half)
     other_half = pl.ds((1 - core) * half, half)
     share_at = core * half + tm_x * share
     own_share = pl.ds(share_at, share)
@@ -117,8 +113,13 @@
             conv.at[c, own_share], conv.at[c, own_share],
             gs.at[n, c, o], gr.at[n, c, o], {"tm": peer * 2 + core})
 
-    def pair_down(n, c):
-        return remote(conv.at[c, own_half], conv.at[c, own_half], qs.at[n, c], qr.at[n, c], partner)
+    def pair_down(n, c, o):
+        held = pl.ds(core * half + lax.rem(tm_x + n_x - o, n_x) * share, share)
+        return remote(conv.at[c, held], conv.at[c, held], qs.at[n, c, o], qr.at[n, c, o], partner)
+
+    def pair_down_recv(n, c):
+        for o in range(n_x):
+            pair_down(n, c, o).wait_recv()
 
     def guess_copy(o):
         return remote(guess, guess_all.at[tm], ds.at[o], dr.at[o], {"tm": lax.rem(tm + o, n_tm)})
@@ -191,7 +192,8 @@
         back_own(n, c).wait()
         if n > 0:
             pair_up(n - 1, c).wait_send()
-            pair_down(n - 1, c).wait_send()
+            for o in range(n_x):
+                pair_down(n - 1, c, o).wait_send()
             for o in range(1, n_x):
                 scatter(n - 1, c, o).wait_send()
                 gather(n - 1, c, o).wait_send()
@@ -230,9 +232,10 @@
 
         for o in range(1, n_x):
             gather(n, c, o).start()
+        pair_down(n, c, 0).start()
         for o in range(1, n_x):
             gather(n, c, o).wait_recv()
-        pair_down(n, c).start()
+            pair_down(n, c, o).start()
 
     def update(n, c):
         for o in range(1, n_mom):
@@ -250,7 +253,7 @@
                     keep_stack(n + 1, k, s, c, new)
 
         some(core * half)
-        pair_down(n, c).wait_recv()
+        pair_down_recv(n, c)
         some((1 - core) * half)
 
     def finish(n):
@@ -272,9 +275,9 @@
                         out[k, s, c] = new[c * group:(c + 1) * group, :]
 
         for c in range(CHUNKS - 1):
-            pair_down(n, c).wait_recv()
+            pair_down_recv(n, c)
         some(core * half)
-        pair_down(n, CHUNKS - 1).wait_recv()
+        pair_down_recv(n, CHUNKS - 1)
         some((1 - core) * half)
 
     first_layout(0)
@@ -287,8 +290,10 @@
         guess_copy(o).start()
     guess_local().start()
 
-    fwd_split[0], fwd_split[1] = split(fwd_table[...])
-    back_split[0], back_split[1] = split(back_table[...])
+    for at, table in enumerate(tables(ordering[...])):
+        fwd_split[0, at * K:(at + 1) * K, :], fwd_split[1, at * K:(at + 1) * K, :] = split(table)
+        turned = split(table.T)
+        back_split[0, :, at * K:(at + 1) * K], back_split[1, :, at * K:(at + 1) * K] = turned
 
     @pl.loop(0, local_k, unroll=4)
     def _(k):
@@ -314,7 +319,8 @@
     n = PASSES - 1
     for c in range(CHUNKS):
         pair_up(n, c).wait_send()
-        pair_down(n, c).wait_send()
+        for o in range(n_x):
+            pair_down(n, c, o).wait_send()
         for o in range(1, n_x):
             scatter(n, c, o).wait_send()
             gather(n, c, o).wait_send()
@@ -325,7 +331,7 @@
         guess_copy(o).wait_send()
 
 
-def panel_step(n_mom, n_tm, start, guess, fwd_table, back_table, wvec, chosen):
+def panel_step(n_mom, n_tm, start, guess, ordering, wvec, chosen):
     local_k = start.shape[0]
     group = start.shape[3]
     rows = group // n_mom
@@ -339,7 +345,7 @@
     return pl.pallas_call(
         functools.partial(step_kernel, n_mom, n_tm),
         out_shape=jax.ShapeDtypeStruct(start.shape, f32),
-        in_specs=[vmem] * 6,
+        in_specs=[vmem] * 5,
         out_specs=vmem,
         scratch_shapes=[
             pltpu.VMEM(panel, f32),
@@ -358,22 +364,19 @@
             dma(many_mom), dma(many_mom), dma(many_mom), dma(many_mom),
             dma(one), dma(one),
             dma(many_x), dma(many_x), dma(many_x), dma(many_x),
-            dma(one), dma(one),
+            dma(many_x), dma(many_x),
             dma((n_tm,)), dma((n_tm,)),
         ],
         compiler_params=pltpu.CompilerParams(
             collective_id=0, has_side_effects=True, vmem_limit_bytes=63 * 1024 * 1024),
         name="panel_step",
-    )(start, guess, fwd_table, back_table, wvec, chosen)
+    )(start, guess, ordering, wvec, chosen)
 
 
 def body(panel_start, block_guess, coupling, slab_owner, expiring, ordering):
     slab_count = lax.axis_size("tm")
     n_mom = lax.axis_size("mom")
     own_index = lax.axis_index("tm")
-    cos_table, sin_table = tables(ordering)
-    fwd_table = jnp.concatenate([cos_table, sin_table], axis=0)
-    back_table = jnp.concatenate([cos_table.T, sin_table.T], axis=1)
     blocks = jnp.arange(slab_count, dtype=jnp.int32)
     slab_mine = jnp.sum(blocks * (slab_owner == own_index).astype(jnp.int32))
     position = (slab_mine - expiring[0]) % slab_count
@@ -386,7 +389,7 @@
     chosen = jnp.broadcast_to((own_index == owner_expiring).astype(jnp.float32), (1, LANES))
     local_k = panel_start.shape[0]
     start = panel_start.reshape(local_k, SPIN, CHUNKS, PANEL // CHUNKS, LANES)
-    result = panel_step(n_mom, slab_count, start, block_guess, fwd_table, back_table, wvec, chosen)
+    result = panel_step(n_mom, slab_count, start, block_guess, ordering[None, :], wvec, chosen)
     return result.reshape(panel_start.shape)
 
 

time: 432 us -> 427 us (0.988)
  other arithmetic: 6.46 us -> 1.93 us
where the time goes in v4:
time: 427 us
  Pallas kernels  417 us (98%)
  local copies, waits for them, and re-layouts  5.31 us (1%)
    pallas_call x1, Pallas kernels, panel_step(): pl.pallas_call(functools.partial(step_kernel, n_mom, n_tm), out_shape=jax...  417 us

profile of v4, /device:TPU:26, one launch (start us, length us, event | category | flops | bytes accessed | tf_op | source)
XLA Modules:
  0.0 426.6 jit_solution(13235028879318406661)
XLA Ops:
  1.3 1.3 fusion.1
  3.8 0.5 broadcast_in_dim.8.chosen
  4.4 0.6 maximum_multiply_fusion.wvec
  5.0 416.9 %panel_step.1 = f32[64,2,2,32,128]{4,3,2,1,0:T(8,128)} custom-call(f32[64,2,2,32,128]{4,3,2,1,0:T(8,128)} %bitcast.10, f32[64,2,16,128]{3,2,1,0:T(8,128)} %guess.1, s32[1,256]{1,0:T(1,128)} %bitcast.11, f32[1,128]{1,0:T(1,128)} %maximum_multiply_fusion.wvec, f32[1,128]{1,0:T(1,128)} %broadcast_in_dim.8.chosen), custom_call_target="tpu_custom_call" | custom-call | tf_op jit(solution)/shard_map/panel_step/pallas_call | solution.py:345
  421.8 4.8 %copy.10 = f32[64,2,64,128]{3,2,1,0:T(8,128)} copy(f32[64,2,64,128]{3,2,1,0:T(8,128)} %bitcast.9) | data formatting | bytes 8388608
  (1 shorter events, 0.0 us)
